TPU v7x, 256 devices: a whole 4x4x8 slice. The times are simulated.
256 devices in a mesh: cell: 16 (over y_hi, z), region: 16 (over x, y_lo, core).
Axes of the slice: x: 4, y: 4 (y_hi: 2, y_lo: 2; y = y_hi * 2 + y_lo), z: 8, core: 2. Of those that a mesh axis runs over, the one named last changes fastest.
Arguments:
- observed: bfloat16 [16384, 65536], P('cell', 'region'), may hold values from -0.5 to 0.5
- block_mask: int32 [2048, 512], P('cell', 'region'), may hold values 0 or 1
- plan: int32 [4], replicated, may hold values from 0 to 3, each once
- cell_factors: float32 [16384, 256], P('cell'), may hold values from -6 to 6
- region_factors: float32 [262144, 256], P(('cell', 'region')), may hold values from -6 to 6
Outputs:
- new_cells: float32 [16384, 256], P('cell')
- new_regions: float32 [262144, 256], P(('cell', 'region'))
Inputs may be any that keep to these rules, and one draw needn't show every extreme that they name: `plan`: each stored slot 0 to 3 appears once.
All inputs are finite; a program needn't handle non-finite values. No bound on the sum of `block_mask` on one device may be relied on, other than what follows from the above.
Results may differ from a plain program's by a relative error of at most 0.0056.
Values sent between devices are 32-bit elements; how exact they have to be, the bound alone decides.
A program may use at most 64 MiB of HBM per device.

v0:
```python
import math

import jax
import jax.numpy as jnp
from jax import lax
from jax.sharding import PartitionSpec as P

STRATA = 4


beta_mom = 0.9


def shifted(value, axis, steps):
    count = lax.axis_size(axis)
    pairs = [(source, (source + steps) % count) for source in range(count)]
    return lax.ppermute(value, axis, pairs)


def body(observed, block_mask, plan, cell_factors, region_factors):
    n_region = lax.axis_size("region")
    cell_rows = cell_factors.shape[0]
    block_rows = region_factors.shape[0]
    total_cols = n_region * block_rows
    scale_pred = 0.5 / math.sqrt(total_cols)
    rate_region = total_cols / cell_rows
    cells_now = cell_factors
    regions_now = region_factors
    momentum = jnp.zeros_like(cell_factors)
    for section in range(STRATA):
        slot_index = plan[section]
        data_block = lax.dynamic_slice_in_dim(observed, slot_index * block_rows, block_rows, 1)
        mask_block = lax.dynamic_slice_in_dim(
            block_mask, slot_index * (block_rows // 128), block_rows // 128, 1
        )
        expanded = jnp.broadcast_to(
            mask_block[:, None, :, None], (cell_rows // 8, 8, block_rows // 128, 128)
        )
        expanded = expanded.reshape(cell_rows, block_rows).astype(jnp.float32)
        cell_bf = cells_now.astype(jnp.bfloat16)
        region_bf = regions_now.astype(jnp.bfloat16)
        predicted = lax.dot_general(
            cell_bf, region_bf, (((1,), (1,)), ((), ())), preferred_element_type=jnp.float32
        )
        resid = (expanded * (scale_pred * predicted - data_block.astype(jnp.float32))).astype(
            jnp.bfloat16
        )
        grad_cell = scale_pred * jnp.dot(resid, region_bf, preferred_element_type=jnp.float32)
        grad_region = scale_pred * lax.dot_general(
            resid, cell_bf, (((0,), (0,)), ((), ())), preferred_element_type=jnp.float32
        )
        regions_now = regions_now - rate_region * grad_region
        grad_total = lax.psum(grad_cell, "region")
        momentum = beta_mom * momentum + grad_total
        cells_now = cells_now - momentum
        if section + 1 < STRATA:
            regions_now = shifted(regions_now, "cell", -1)
    regions_now = shifted(regions_now, "cell", STRATA - 1)
    return (cells_now, regions_now)


def solution(mesh):
    in_specs = (
        P("cell", "region"),
        P("cell", "region"),
        P(),
        P("cell", None),
        P(("cell", "region"), None),
    )
    out_specs = (P("cell", None), P(("cell", "region"), None))
    return jax.shard_map(body, mesh=mesh, in_specs=in_specs, out_specs=out_specs, check_vma=False)
```

profile of v0, /device:TPU:73, one launch (start us, length us, event | category | flops | bytes accessed | tf_op | source)
XLA Modules:
  0.0 585.5 jit_solution(13548433549725169644)
XLA Ops:
  7.2 1.4 fusion.26
  11.8 0.7 dynamic-slice_convert_fusion
  12.5 0.1 copy.7
  12.6 3.1 fusion.3
  15.8 1.7 convolution_multiply_fusion.7
  17.5 2.9 fusion.7
  21.1 0.1 copy.8
  21.2 131.7 %all-reduce.5.cloned.1.call-done = f32[1024,256]{1,0:T(8,128)} async-done(((f32[1024,256]{1,0:T(8,128)}), f32[1024,256]{1,0:T(8,128)}) %all-reduce.5.cloned.1.call-update) | async-done | bytes 1048592 | tf_op jit(solution)/shard_map/psum | solution.py:53
  152.9 1.7 sub.37
  154.6 3.6 fusion.2
  158.2 2.9 convolution_multiply_fusion.5
  161.1 0.0 all-reduce.9.cloned.1.call-start
  161.2 2.9 fusion.6
  164.1 0.2 collective-permute-start.1
  164.9 0.1 copy.9
  165.0 130.9 %all-reduce.7.cloned.1.call-done = f32[1024,256]{1,0:T(8,128)} async-done(((f32[1024,256]{1,0:T(8,128)}), f32[1024,256]{1,0:T(8,128)}) %all-reduce.7.cloned.1.call-update) | async-done | bytes 1048592 | tf_op jit(solution)/shard_map/psum | solution.py:53
  295.9 1.7 fusion.8
  297.6 3.6 fusion.1
  301.3 2.9 convolution_multiply_fusion.3
  304.2 0.0 all-reduce.11.cloned.1.call-start
  304.2 2.9 fusion.5
  307.2 0.2 collective-permute-start.2
  308.0 0.1 copy.10
  308.1 130.8 %all-reduce.9.cloned.1.call-done = f32[1024,256]{1,0:T(8,128)} async-done(((f32[1024,256]{1,0:T(8,128)}), f32[1024,256]{1,0:T(8,128)}) %all-reduce.9.cloned.1.call-update) | async-done | bytes 1048592 | tf_op jit(solution)/shard_map/psum | solution.py:53
  438.9 2.1 fusion.25
  441.0 3.6 fusion
  444.7 2.9 convolution_multiply_fusion.1
  447.6 3.0 fusion.4
  450.6 3.6 collective-permute-start.3
  454.1 120.3 %all-reduce.11.cloned.1.call-done = f32[1024,256]{1,0:T(8,128)} async-done(((f32[1024,256]{1,0:T(8,128)}), f32[1024,256]{1,0:T(8,128)}) %all-reduce.11.cloned.1.call-update) | async-done | bytes 1048592 | tf_op jit(solution)/shard_map/psum | solution.py:53
  574.5 3.5 add_subtract_fusion
  578.0 1.0 copy.16
  (13 shorter events, 0.2 us)
Async XLA Ops:
  7.2 145.7 %all-reduce.5.cloned.1.call-start = ((), (), s32[]{:S(2)}) async-start(), calls=%async_computation | async-start | bytes 2097152 | tf_op jit(solution)/shard_map/psum | solution.py:53
  12.6 3.1 copy-start
  17.5 278.4 %all-reduce.7.cloned.1.call-start = ((), (), s32[]{:S(2)}) async-start(), calls=%async_computation.1 | async-start | bytes 2097152 | tf_op jit(solution)/shard_map/psum | solution.py:53
  20.5 134.1 %collective-permute-start = (f32[1024,256]{1,0:T(8,128)}, f32[1024,256]{1,0:T(8,128)}, u32[]{:S(2)}, u32[]{:S(2)}) collective-permute-start(f32[1024,256]{1,0:T(8,128)} %fusion.7), channel_id=1, source_target_pairs={{0,240},{16,0},{32,16},{48,32},{64,48},{80,64},{96,80},{112,96},{1... | collective-permute-start | bytes 3145736 | tf_op jit(solution)/shard_map/ppermute | solution.py:17
  161.1 277.8 %all-reduce.9.cloned.1.call-start = ((), (), s32[]{:S(2)}) async-start(), calls=%async_computation.2 | async-start | bytes 2097152 | tf_op jit(solution)/shard_map/psum | solution.py:53
  164.1 133.5 %collective-permute-start.1 = (f32[1024,256]{1,0:T(8,128)}, f32[1024,256]{1,0:T(8,128)}, u32[]{:S(2)}, u32[]{:S(2)}) collective-permute-start(f32[1024,256]{1,0:T(8,128)} %fusion.6), channel_id=1, source_target_pairs={{0,240},{16,0},{32,16},{48,32},{64,48},{80,64},{96,80},{112,96},{1... | collective-permute-start | bytes 3145736 | tf_op jit(solution)/shard_map/ppermute | solution.py:17
  304.2 270.3 %all-reduce.11.cloned.1.call-start = ((), (), s32[]{:S(2)}) async-start(), calls=%async_computation.3 | async-start | bytes 2097152 | tf_op jit(solution)/shard_map/psum | solution.py:53
  307.2 133.8 %collective-permute-start.2 = (f32[1024,256]{1,0:T(8,128)}, f32[1024,256]{1,0:T(8,128)}, u32[]{:S(2)}, u32[]{:S(2)}) collective-permute-start(f32[1024,256]{1,0:T(8,128)} %fusion.5), channel_id=1, source_target_pairs={{0,240},{16,0},{32,16},{48,32},{64,48},{80,64},{96,80},{112,96},{1... | collective-permute-start | bytes 3145736 | tf_op jit(solution)/shard_map/ppermute | solution.py:17
  450.6 127.4 %collective-permute-start.3 = (f32[1024,256]{1,0:T(8,128)}, f32[1024,256]{1,0:T(8,128)S(1)}, u32[]{:S(2)}, u32[]{:S(2)}) collective-permute-start(f32[1024,256]{1,0:T(8,128)} %fusion.4), channel_id=1, source_target_pairs={{0,48},{16,64},{32,80},{48,96},{64,112},{80,128},{96,144},{112,160... | collective-permute-start | bytes 3145736 | tf_op jit(solution)/shard_map/ppermute | solution.py:17
Sparse Core Ops, SparseCore 0:
  17.6 135.2 all-reduce.4
  161.2 134.6 all-reduce.6
  304.3 134.5 all-reduce.8
  447.7 126.7 all-reduce.10
where the time goes:
time: 591 us; the launch traced here: 585 us
  waiting for transfers between devices  514 us (87%)
  matrix products  36.2 us (6%)
  between operations  18.8 us (3%)
  other arithmetic  9.77 us (2%)
    psum x4, waiting for transfers between devices, body(): grad_total = lax.psum(grad_cell, 'region')  514 us
    dot_general x4, matrix products, body(): lax.dot_general(cell_bf, region_bf, (((1,), (1,)), ((), ())), preferred_e...  13.9 us
  transfers between devices with their start and end apart: 8, of which 4 were waited for; matrix products, arithmetic and copies ran while one was open for 4% of the time, Pallas kernels for 0%

commit v1 on v0

v1 whole, which is shorter than its diff:
```python
import functools
import math

import jax
import jax.numpy as jnp
from jax import lax
from jax.experimental import pallas as pl
from jax.experimental.pallas import tpu as pltpu
from jax.sharding import PartitionSpec as P

STRATA = 4
MOMENTUM = 0.9
ROWS = 1024
RANK = 256
CHUNK = 256
CHUNKS = ROWS // CHUNK
HALF = ROWS // 2
PIECE = 64
RET = 128
RETS = ROWS // RET
DOWN = (0, 2, 4)
RAW, FINAL, TURN, RELAY = 4, 7, 8, 9
NT = (((1,), (1,)), ((), ()))
TN = (((0,), (0,)), ((), ()))


def remote(src, dst, send, recv, cell, region):
    return pltpu.make_async_remote_copy(
        src_ref=src,
        dst_ref=dst,
        send_sem=send,
        recv_sem=recv,
        device_id={"cell": cell, "region": region},
        device_id_type=pl.DeviceIdType.MESH,
    )


def kernel(
    scale, rate, plan, mask, y_hbm, u_hbm, v_hbm, out_u, out_v,
    ybuf, vbuf, ubuf, gbuf, core_buf, sum_buf, expanded, resid, u_bf, u_scaled, moment,
    load_sem, shift_send, shift_recv, pass_send,
    core_send, core_recv, rs_send, rs_recv, ag_send, ag_recv, agc_send, agc_recv,
    ret_send, ret_recv, relay_send, relay_recv, turn_send, turn_recv, out_sem,
):
    cell, region = lax.axis_index("cell"), lax.axis_index("region")
    z, core, chip = cell % 8, region % 2, region // 2
    ring = cell - z
    across = (cell + 8) % 16
    other_core = region + 1 - 2 * core

    def along(steps):
        return ring + (z + steps + 8) % 8

    def peer(d):
        return ((chip + d) % 8) * 2 + core

    def v_rows(slot, k):
        return vbuf.at[slot, pl.ds(k * CHUNK, CHUNK)]

    def ret_rows(slot, p):
        return vbuf.at[slot, pl.ds(p * RET, RET)]

    loads = [
        pltpu.make_async_copy(u_hbm, ubuf.at[0], load_sem.at[0]),
        pltpu.make_async_copy(v_hbm, vbuf.at[0], load_sem.at[1]),
    ] + [
        pltpu.make_async_copy(y_hbm.at[:, pl.ds(q * ROWS, ROWS)], ybuf.at[q], load_sem.at[2 + q]) for q in range(STRATA)
    ]
    for load in loads:
        load.start()

    barrier = pltpu.get_barrier_semaphore()
    greeted = [(cell, other_core)] + [(cell, peer(d)) for d in range(1, 8)]
    greeted += [(along(d), region) for d in (-1, 1, -3, 3, -2, 2)] + [(across, region)]
    for c, r in greeted:
        pl.semaphore_signal(
            barrier, inc=1, device_id={"cell": c, "region": r}, device_id_type=pl.DeviceIdType.MESH
        )
    moment[...] = jnp.zeros_like(moment)
    mask_bf = mask[...].astype(jnp.float32).astype(jnp.bfloat16)
    block = lax.broadcasted_iota(jnp.int32, (32, ROWS), 0)
    lane = lax.broadcasted_iota(jnp.int32, (32, ROWS), 1)
    for q in range(STRATA):
        chosen = (block == q * 8 + lane // 128).astype(jnp.float32).astype(jnp.bfloat16)
        expanded[q] = jnp.dot(mask_bf, chosen, preferred_element_type=jnp.float32)
    for load in loads:
        load.wait()
    pl.semaphore_wait(barrier, len(greeted))

    is0 = 1 - (z + 7) // 8
    mine = core * HALF + chip * PIECE

    def shift_copy(s, k):
        slot = s + 1 + is0 * (RAW - 1)
        first = along(-1)
        to = first if k < 2 else first + is0 * (across - first)
        return remote(v_rows(s, k), v_rows(slot, k), shift_send.at[s, k], shift_recv.at[slot, k], to, region)

    def shift_copy_in(s, k):
        remote(v_rows(s, k), v_rows(s, k), shift_send.at[0, k], shift_recv.at[s, k], cell, region).wait_recv()

    def pass_on(s, k, to):
        remote(v_rows(RAW + s, k), v_rows(RAW + s, k), pass_send.at[s, k], shift_recv.at[RAW + s, k], to, region).wait_recv()
        remote(v_rows(RAW + s, k), v_rows(s + 1, k), pass_send.at[s, k], shift_recv.at[s + 1, k], to, region).start()

    def pass_wait(s, k, to):
        remote(v_rows(RAW + s, k), v_rows(s + 1, k), pass_send.at[s, k], shift_recv.at[s + 1, k], to, region).wait_send()

    def ret_copy(p):
        slot = FINAL + (z + 3) // 8
        return remote(ret_rows(3, p), ret_rows(slot, p), ret_send.at[p], ret_recv.at[slot - FINAL, p], along(3), region)

    def ret_copy_down(p):
        return remote(ret_rows(3, p), ret_rows(RELAY, p), ret_send.at[p], relay_recv.at[p], along(-3), region)

    def relay_copy(p):
        source = (z + 3) % 8
        slot = FINAL + (source + 3) // 8
        return remote(ret_rows(RELAY, p), ret_rows(slot, p), relay_send.at[p], ret_recv.at[slot - FINAL, p], along(-2), region)

    def turn_copy(p):
        return remote(ret_rows(TURN, p), ret_rows(FINAL, p), turn_send.at[p], ret_recv.at[0, p], across, region)

    def core_copy(s):
        away = pl.ds((1 - core) * HALF, HALF)
        return remote(gbuf.at[s, away], core_buf.at[s], core_send.at[s], core_recv.at[s], cell, other_core)

    def rs_copy(s, d):
        rows = pl.ds(core * HALF + ((chip + d) % 8) * PIECE, PIECE)
        return remote(gbuf.at[s, rows], sum_buf.at[s, d], rs_send.at[s, d], rs_recv.at[s, d], cell, peer(d))

    def ag_copy(s, d):
        rows = pl.ds(mine, PIECE)
        return remote(ubuf.at[s + 1, rows], ubuf.at[s + 1, rows], ag_send.at[s, d], ag_recv.at[s, d], cell, peer(d))

    def agc_copy(s, d):
        rows = pl.ds(core * HALF + ((chip - d + 8) % 8) * PIECE, PIECE)
        return remote(ubuf.at[s + 1, rows], ubuf.at[s + 1, rows], agc_send.at[s, d], agc_recv.at[s, d], cell, other_core)

    def prepare(s):
        u = ubuf[s].astype(jnp.bfloat16)
        u_bf[...] = u
        u_scaled[...] = u * jnp.bfloat16(scale)

    def chunk(s, k):
        v_bf = vbuf[s, pl.ds(k * CHUNK, CHUNK), :].astype(jnp.bfloat16)
        q, columns = plan[s], pl.ds(k * CHUNK, CHUNK)
        for m in range(4):
            base = pl.multiple_of(((1 - core) * HALF + m * 256) % ROWS, 256)
            rows = pl.ds(base, 256)
            predicted = lax.dot_general(u_scaled[rows, :], v_bf, NT, preferred_element_type=jnp.float32)
            w = expanded[q, pl.ds(pl.multiple_of(base // 8, 32), 32), columns]
            w = jnp.broadcast_to(w[:, None, :], (32, 8, CHUNK)).reshape(256, CHUNK)
            r = (w * (predicted - ybuf[q, rows, columns].astype(jnp.float32))).astype(jnp.bfloat16)
            resid[rows, :] = r
            g = scale * jnp.dot(r, v_bf, preferred_element_type=jnp.float32)
            gbuf[s, rows, :] = g if k == 0 else gbuf[s, rows, :] + g
            if k == CHUNKS - 1 and m == 1:
                core_copy(s).start()
        h = scale * lax.dot_general(resid[...], u_bf[...], TN, preferred_element_type=jnp.float32)
        vbuf[s, pl.ds(k * CHUNK, CHUNK), :] = vbuf[s, pl.ds(k * CHUNK, CHUNK), :] - rate * h

    def reduce_core(s):
        core_copy(s).wait_recv()
        own = pl.ds(pl.multiple_of(core * HALF, HALF), HALF)
        gbuf[s, own, :] = gbuf[s, own, :] + core_buf[s]
        for d in (4, 3, 5, 2, 6, 1, 7):
            rs_copy(s, d).start()

    def reduce_chips(s):
        rows = pl.ds(pl.multiple_of(mine, PIECE), PIECE)
        total = gbuf[s, rows, :]
        for d in range(1, 8):
            rs_copy(s, d).wait_recv()
            total = total + sum_buf[s, d]
        step = MOMENTUM * moment[...] + total
        moment[...] = step
        ubuf[s + 1, rows, :] = ubuf[s, rows, :] - step
        for d in (4, 3, 5, 2, 6, 1, 7):
            ag_copy(s, d).start()
        agc_copy(s, 0).start()

    def gather(s):
        for d in range(1, 8):
            ag_copy(s, d).wait_recv()
            agc_copy(s, d).start()
        for d in range(8):
            agc_copy(s, d).wait_recv()

    @pl.loop(0, STRATA - 1)
    def _(s):
        prepare(s)
        for k in range(CHUNKS):
            @pl.when(s > 0)
            def _():
                shift_copy_in(s, k)
            chunk(s, k)
            shift_copy(s, k).start()
        reduce_core(s)

        @pl.when(z == 7)
        def _():
            pass_on(s, 0, across)

        @pl.when(z == 0)
        def _():
            pass_on(s, 2, along(-1))
            pass_on(s, 3, along(-1))

        reduce_chips(s)

        @pl.when(z == 7)
        def _():
            pass_on(s, 1, across)

        gather(s)

    s = STRATA - 1
    prepare(s)
    for k in range(CHUNKS):
        shift_copy_in(s, k)
        chunk(s, k)
        for p in (2 * k, 2 * k + 1):
            (ret_copy_down(p) if p in DOWN else ret_copy(p)).start()
    reduce_core(s)

    def relay(p):
        ret_copy_down(p).wait_recv()
        relay_copy(p).start()

    relay(DOWN[0])
    reduce_chips(s)
    relay(DOWN[1])
    gather(s)
    store_u = pltpu.make_async_copy(ubuf.at[STRATA], out_u, out_sem.at[RETS])
    store_u.start()
    relay(DOWN[2])

    order = (1, 3, 0, 5, 2, 6, 4, 7)

    @pl.when(z < 3)
    def _():
        for p in order:
            remote(ret_rows(TURN, p), ret_rows(TURN, p), ret_send.at[p], ret_recv.at[1, p], cell, region).wait_recv()
            turn_copy(p).start()

    stores = []
    for p in order:
        remote(ret_rows(FINAL, p), ret_rows(FINAL, p), ret_send.at[p], ret_recv.at[0, p], cell, region).wait_recv()
        store = pltpu.make_async_copy(vbuf.at[FINAL, pl.ds(p * RET, RET)], out_v.at[pl.ds(p * RET, RET)], out_sem.at[p])
        store.start()
        stores.append(store)

    @pl.loop(0, STRATA)
    def _(s):
        core_copy(s).wait_send()
        for d in range(1, 8):
            rs_copy(s, d).wait_send()
            ag_copy(s, d).wait_send()
        for d in range(8):
            agc_copy(s, d).wait_send()

    @pl.loop(0, STRATA - 1)
    def _(s):
        for k in range(CHUNKS):
            shift_copy(s, k).wait_send()

        @pl.when(z == 7)
        def _():
            pass_wait(s, 0, across)
            pass_wait(s, 1, across)

        @pl.when(z == 0)
        def _():
            pass_wait(s, 2, along(-1))
            pass_wait(s, 3, along(-1))

    for p in range(RETS):
        (ret_copy_down(p) if p in DOWN else ret_copy(p)).wait_send()
    for p in DOWN:
        relay_copy(p).wait_send()

    @pl.when(z < 3)
    def _():
        for p in order:
            turn_copy(p).wait_send()

    store_u.wait()
    for store in stores:
        store.wait()


def body(observed, block_mask, plan, cell_factors, region_factors):
    total_cols = lax.axis_size("region") * ROWS
    scale = 0.5 / math.sqrt(total_cols)
    rate = total_cols / ROWS
    dma = pltpu.SemaphoreType.DMA
    f32, bf16 = jnp.float32, jnp.bfloat16
    anywhere = pl.BlockSpec(memory_space=pl.ANY)
    out = jax.ShapeDtypeStruct((ROWS, RANK), f32)
    return pl.pallas_call(
        functools.partial(kernel, scale, rate),
        name="epoch",
        out_shape=(out, out),
        in_specs=[
            pl.BlockSpec(memory_space=pltpu.SMEM),
            pl.BlockSpec(memory_space=pltpu.VMEM),
            anywhere,
            anywhere,
            anywhere,
        ],
        out_specs=(anywhere, anywhere),
        scratch_shapes=[
            pltpu.VMEM((STRATA, ROWS, ROWS), bf16),
            pltpu.VMEM((10, ROWS, RANK), f32),
            pltpu.VMEM((STRATA + 1, ROWS, RANK), f32),
            pltpu.VMEM((STRATA, ROWS, RANK), f32),
            pltpu.VMEM((STRATA, HALF, RANK), f32),
            pltpu.VMEM((STRATA, 8, PIECE, RANK), f32),
            pltpu.VMEM((STRATA, ROWS // 8, ROWS), f32),
            pltpu.VMEM((ROWS, CHUNK), bf16),
            pltpu.VMEM((ROWS, RANK), bf16),
            pltpu.VMEM((ROWS, RANK), bf16),
            pltpu.VMEM((PIECE, RANK), f32),
            dma((2 + STRATA,)),
            dma((3, CHUNKS)),
            dma((7, CHUNKS)),
            dma((3, CHUNKS)),
            dma((STRATA,)),
            dma((STRATA,)),
            dma((STRATA, 8)),
            dma((STRATA, 8)),
            dma((STRATA, 8)),
            dma((STRATA, 8)),
            dma((STRATA, 8)),
            dma((STRATA, 8)),
            dma((RETS,)),
            dma((2, RETS)),
            dma((RETS,)),
            dma((RETS,)),
            dma((RETS,)),
            dma((RETS,)),
            dma((RETS + 1,)),
        ],
        compiler_params=pltpu.CompilerParams(
            collective_id=0, has_side_effects=True, vmem_limit_bytes=56 * 2**20
        ),
    )(plan, block_mask, observed, cell_factors, region_factors)


def solution(mesh):
    in_specs = (
        P("cell", "region"),
        P("cell", "region"),
        P(),
        P("cell", None),
        P(("cell", "region"), None),
    )
    out_specs = (P("cell", None), P(("cell", "region"), None))
    return jax.shard_map(body, mesh=mesh, in_specs=in_specs, out_specs=out_specs, check_vma=False)
```

time: 591 us -> 164 us (0.28)
  waiting for transfers between devices: 514 us -> 0 us
  Pallas kernels: 0 us -> 156 us
  matrix products: 36.2 us -> 0 us
  between operations: 18.8 us -> 0.64 us
  other arithmetic: 9.77 us -> 0 us
    psum x4 -> x0, waiting for transfers between devices: 514 us -> none  [body(): grad_total = lax.psum(grad_cell, 'region')]
    pallas_call x0 -> x1, Pallas kernels: none -> 156 us  [body(): pl.pallas_call(functools.partial(kernel, scale, rate), name='epoch', out_...]
    dot_general x12 -> x0, matrix products: 36.2 us -> none  [the longest x4 13.9 us: body(): lax.dot_general(cell_bf, region_bf, (((1,), (1,)), ((), ())), preferred_e...]
    sub x4 -> x0, other arithmetic: 9.02 us -> none  [body(): cells_now = cells_now - momentum]
  transfers between devices with their start and end apart: 8 -> 0, of which waited for: 4 -> 0; matrix products, arithmetic and copies ran while one was open for 4% -> 0% of each run, Pallas kernels for 0% -> 0%
where the time goes in v1:
time: 164 us; the launch traced here: 163 us
  Pallas kernels  156 us (95%)
  local copies, waits for them, and re-layouts  5.97 us (4%)
    pallas_call x1, Pallas kernels, body(): pl.pallas_call(functools.partial(kernel, scale, rate), name='epoch', out_...  156 us
    unnamed x3, local copies, waits for them, and re-layouts  5.97 us

profile of v1, /device:TPU:73, one launch (start us, length us, event | category | flops | bytes accessed | tf_op | source)
XLA Modules:
  0.0 162.6 jit_solution(1137031325878658684)
XLA Ops:
  0.6 1.4 copy.7.mask
  2.1 156.0 %epoch.1 = (f32[1024,256]{1,0:T(8,128)}, f32[1024,256]{1,0:T(8,128)}) custom-call(s32[4]{0:T(128)} %plan.1, s32[128,32]{1,0:T(8,128)} %copy.7.mask, bf16[1024,4096]{1,0:T(8,128)(2,1)} %y_hbm.1, f32[1024,256]{1,0:T(8,128)} %u_hbm.1, f32[1024,256]{1,0:T(8,128)} %v_hbm.1), custom_call_target="tpu_custom_call" | custom-call | tf_op jit(solution)/shard_map/epoch/pallas_call | solution.py:301
  158.0 2.3 %copy.10 = f32[1024,256]{1,0:T(8,128)} copy(f32[1024,256]{1,0:T(8,128)} %get-tuple-element.4) | data formatting | bytes 2097152
  160.3 2.3 %copy.11 = f32[1024,256]{1,0:T(8,128)} copy(f32[1024,256]{1,0:T(8,128)} %get-tuple-element.5) | data formatting | bytes 2097152

commit v2 on v1

--- a/solution.py
+++ b/solution.py
@@ -19,7 +19,7 @@
 RET = 128
 RETS = ROWS // RET
 DOWN = (0, 2, 4)
-RAW, FINAL, TURN, RELAY = 4, 7, 8, 9
+RAW, FINAL, RELAY = 4, 7, 8
 NT = (((1,), (1,)), ((), ()))
 TN = (((0,), (0,)), ((), ()))
 
@@ -40,7 +40,7 @@
     ybuf, vbuf, ubuf, gbuf, core_buf, sum_buf, expanded, resid, u_bf, u_scaled, moment,
     load_sem, shift_send, shift_recv, pass_send,
     core_send, core_recv, rs_send, rs_recv, ag_send, ag_recv, agc_send, agc_recv,
-    ret_send, ret_recv, relay_send, relay_recv, turn_send, turn_recv, out_sem,
+    ret_send, ret_recv, relay_send, relay_recv,
 ):
     cell, region = lax.axis_index("cell"), lax.axis_index("region")
     z, core, chip = cell % 8, region % 2, region // 2
@@ -51,8 +51,11 @@
     def along(steps):
         return ring + (z + steps + 8) % 8
 
+    x, y = chip // 2, chip % 2
+    level = region + 2 - 4 * y
+
     def peer(d):
-        return ((chip + d) % 8) * 2 + core
+        return (region + 4 * d) % 16
 
     def v_rows(slot, k):
         return vbuf.at[slot, pl.ds(k * CHUNK, CHUNK)]
@@ -70,8 +73,12 @@
         load.start()
 
     barrier = pltpu.get_barrier_semaphore()
-    greeted = [(cell, other_core)] + [(cell, peer(d)) for d in range(1, 8)]
-    greeted += [(along(d), region) for d in (-1, 1, -3, 3, -2, 2)] + [(across, region)]
+    greeted = [(cell, other_core)] + [(cell, level)] + [(cell, peer(d)) for d in (1, 2, 3)]
+    greeted += [(along(d), region) for d in (-1, 1, -3, 3)] + [(across, region)]
+    last = (cell + 13) % 16
+    sender = last - last % 8 + (last % 8 + 5) % 8
+    greeted += [((cell + 3) % 16, region), ((along(3) + 3) % 16, region)]
+    greeted += [(last, region), (sender, region)]
     for c, r in greeted:
         pl.semaphore_signal(
             barrier, inc=1, device_id={"cell": c, "region": r}, device_id_type=pl.DeviceIdType.MESH
@@ -82,7 +89,7 @@
     lane = lax.broadcasted_iota(jnp.int32, (32, ROWS), 1)
     for q in range(STRATA):
         chosen = (block == q * 8 + lane // 128).astype(jnp.float32).astype(jnp.bfloat16)
-        expanded[q] = jnp.dot(mask_bf, chosen, preferred_element_type=jnp.float32)
+        expanded[q] = lax.dot_general(mask_bf, chosen, TN, preferred_element_type=jnp.float32)
     for load in loads:
         load.wait()
     pl.semaphore_wait(barrier, len(greeted))
@@ -107,35 +114,51 @@
         remote(v_rows(RAW + s, k), v_rows(s + 1, k), pass_send.at[s, k], shift_recv.at[s + 1, k], to, region).wait_send()
 
     def ret_copy(p):
-        slot = FINAL + (z + 3) // 8
-        return remote(ret_rows(3, p), ret_rows(slot, p), ret_send.at[p], ret_recv.at[slot - FINAL, p], along(3), region)
+        return remote(ret_rows(3, p), ret_rows(FINAL, p), ret_send.at[p], ret_recv.at[p], (cell + 3) % 16, region)
 
     def ret_copy_down(p):
         return remote(ret_rows(3, p), ret_rows(RELAY, p), ret_send.at[p], relay_recv.at[p], along(-3), region)
 
     def relay_copy(p):
-        source = (z + 3) % 8
-        slot = FINAL + (source + 3) // 8
-        return remote(ret_rows(RELAY, p), ret_rows(slot, p), relay_send.at[p], ret_recv.at[slot - FINAL, p], along(-2), region)
-
-    def turn_copy(p):
-        return remote(ret_rows(TURN, p), ret_rows(FINAL, p), turn_send.at[p], ret_recv.at[0, p], across, region)
+        home = (along(3) + 3) % 16
+        return remote(ret_rows(RELAY, p), ret_rows(FINAL, p), relay_send.at[p], ret_recv.at[p], home, region)
+
+    def ret_in(p):
+        rows = ret_rows(FINAL, p)
+        return remote(rows, rows, ret_send.at[p], ret_recv.at[p], cell, region)
 
     def core_copy(s):
         away = pl.ds((1 - core) * HALF, HALF)
         return remote(gbuf.at[s, away], core_buf.at[s], core_send.at[s], core_recv.at[s], cell, other_core)
 
-    def rs_copy(s, d):
-        rows = pl.ds(core * HALF + ((chip + d) % 8) * PIECE, PIECE)
-        return remote(gbuf.at[s, rows], sum_buf.at[s, d], rs_send.at[s, d], rs_recv.at[s, d], cell, peer(d))
-
-    def ag_copy(s, d):
-        rows = pl.ds(mine, PIECE)
-        return remote(ubuf.at[s + 1, rows], ubuf.at[s + 1, rows], ag_send.at[s, d], ag_recv.at[s, d], cell, peer(d))
-
-    def agc_copy(s, d):
-        rows = pl.ds(core * HALF + ((chip - d + 8) % 8) * PIECE, PIECE)
-        return remote(ubuf.at[s + 1, rows], ubuf.at[s + 1, rows], agc_send.at[s, d], agc_recv.at[s, d], cell, other_core)
+    def piece(px, py):
+        return pl.ds(core * HALF + ((px + 4) % 4 * 2 + py) * PIECE, PIECE)
+
+    def rs_copy(s, far, d):
+        i = 3 * far + d - 1
+        rows = piece(x + d, y + far - 2 * far * y)
+        return remote(gbuf.at[s, rows], sum_buf.at[s, i], rs_send.at[s, i], rs_recv.at[s, i], cell, peer(d))
+
+    def rs_copy_y(s):
+        rows = piece(x, 1 - y)
+        return remote(gbuf.at[s, rows], sum_buf.at[s, 6], rs_send.at[s, 6], rs_recv.at[s, 6], cell, level)
+
+    def ag_copy(s, i, px, py, to):
+        rows = ubuf.at[s + 1, piece(px, py)]
+        return remote(rows, rows, ag_send.at[s, i], ag_recv.at[s, i], cell, to)
+
+    def ag_near(s, d):
+        return ag_copy(s, d - 1, x, y, peer(d))
+
+    def ag_far(s, d):
+        return ag_copy(s, 2 + d, x, 1 - y, peer(d))
+
+    def ag_y(s):
+        return ag_copy(s, 6, x, y, level)
+
+    def agc_copy(s, i, px, py):
+        rows = ubuf.at[s + 1, piece(px, py)]
+        return remote(rows, rows, agc_send.at[s, i], agc_recv.at[s, i], cell, other_core)
 
     def prepare(s):
         u = ubuf[s].astype(jnp.bfloat16)
@@ -164,28 +187,52 @@
         core_copy(s).wait_recv()
         own = pl.ds(pl.multiple_of(core * HALF, HALF), HALF)
         gbuf[s, own, :] = gbuf[s, own, :] + core_buf[s]
-        for d in (4, 3, 5, 2, 6, 1, 7):
-            rs_copy(s, d).start()
-
-    def reduce_chips(s):
-        rows = pl.ds(pl.multiple_of(mine, PIECE), PIECE)
+        for far in (1, 0):
+            for d in (2, 1, 3):
+                rs_copy(s, far, d).start()
+
+    def aligned(px, py):
+        return pl.ds(pl.multiple_of(core * HALF + (px * 2 + py) * PIECE, PIECE), PIECE)
+
+    def reduce_far(s):
+        rows = aligned(x, 1 - y)
         total = gbuf[s, rows, :]
-        for d in range(1, 8):
-            rs_copy(s, d).wait_recv()
-            total = total + sum_buf[s, d]
-        step = MOMENTUM * moment[...] + total
+        for d in (1, 3, 2):
+            rs_copy(s, 1, d).wait_recv()
+            total = total + sum_buf[s, 2 + d]
+        gbuf[s, rows, :] = total
+        rs_copy_y(s).start()
+
+    def reduce_near(s):
+        rows = aligned(x, y)
+        total = gbuf[s, rows, :]
+        for d in (1, 3, 2):
+            rs_copy(s, 0, d).wait_recv()
+            total = total + sum_buf[s, d - 1]
+        rs_copy_y(s).wait_recv()
+        step = MOMENTUM * moment[...] + (total + sum_buf[s, 6])
         moment[...] = step
         ubuf[s + 1, rows, :] = ubuf[s, rows, :] - step
-        for d in (4, 3, 5, 2, 6, 1, 7):
-            ag_copy(s, d).start()
-        agc_copy(s, 0).start()
+        ag_y(s).start()
+        for d in (2, 1, 3):
+            ag_near(s, d).start()
+        agc_copy(s, 6, x, y).start()
+
+    def gather_y(s):
+        ag_y(s).wait_recv()
+        for d in (2, 1, 3):
+            ag_far(s, d).start()
+        agc_copy(s, 7, x, 1 - y).start()
 
     def gather(s):
-        for d in range(1, 8):
-            ag_copy(s, d).wait_recv()
-            agc_copy(s, d).start()
-        for d in range(8):
-            agc_copy(s, d).wait_recv()
+        for d in (1, 3, 2):
+            ag_near(s, d).wait_recv()
+            agc_copy(s, d - 1, x - d, y).start()
+        for d in (1, 3, 2):
+            ag_far(s, d).wait_recv()
+            agc_copy(s, 2 + d, x - d, 1 - y).start()
+        for i in range(8):
+            agc_copy(s, i, x, y).wait_recv()
 
     @pl.loop(0, STRATA - 1)
     def _(s):
@@ -197,6 +244,7 @@
             chunk(s, k)
             shift_copy(s, k).start()
         reduce_core(s)
+        reduce_far(s)
 
         @pl.when(z == 7)
         def _():
@@ -205,13 +253,18 @@
         @pl.when(z == 0)
         def _():
             pass_on(s, 2, along(-1))
+
+        reduce_near(s)
+
+        @pl.when(z == 7)
+        def _():
+            pass_on(s, 1, across)
+
+        gather_y(s)
+
+        @pl.when(z == 0)
+        def _():
             pass_on(s, 3, along(-1))
-
-        reduce_chips(s)
-
-        @pl.when(z == 7)
-        def _():
-            pass_on(s, 1, across)
 
         gather(s)
 
@@ -228,37 +281,33 @@
         ret_copy_down(p).wait_recv()
         relay_copy(p).start()
 
+    reduce_far(s)
     relay(DOWN[0])
-    reduce_chips(s)
+    reduce_near(s)
+    gather_y(s)
     relay(DOWN[1])
     gather(s)
-    store_u = pltpu.make_async_copy(ubuf.at[STRATA], out_u, out_sem.at[RETS])
-    store_u.start()
+    out_u[...] = ubuf[STRATA]
     relay(DOWN[2])
 
     order = (1, 3, 0, 5, 2, 6, 4, 7)
 
-    @pl.when(z < 3)
-    def _():
-        for p in order:
-            remote(ret_rows(TURN, p), ret_rows(TURN, p), ret_send.at[p], ret_recv.at[1, p], cell, region).wait_recv()
-            turn_copy(p).start()
-
-    stores = []
     for p in order:
-        remote(ret_rows(FINAL, p), ret_rows(FINAL, p), ret_send.at[p], ret_recv.at[0, p], cell, region).wait_recv()
-        store = pltpu.make_async_copy(vbuf.at[FINAL, pl.ds(p * RET, RET)], out_v.at[pl.ds(p * RET, RET)], out_sem.at[p])
-        store.start()
-        stores.append(store)
+        ret_in(p).wait_recv()
+        out_v[pl.ds(p * RET, RET), :] = vbuf[FINAL, pl.ds(p * RET, RET), :]
 
     @pl.loop(0, STRATA)
     def _(s):
         core_copy(s).wait_send()
-        for d in range(1, 8):
-            rs_copy(s, d).wait_send()
-            ag_copy(s, d).wait_send()
-        for d in range(8):
-            agc_copy(s, d).wait_send()
+        rs_copy_y(s).wait_send()
+        ag_y(s).wait_send()
+        for d in (1, 2, 3):
+            rs_copy(s, 0, d).wait_send()
+            rs_copy(s, 1, d).wait_send()
+            ag_near(s, d).wait_send()
+            ag_far(s, d).wait_send()
+        for i in range(8):
+            agc_copy(s, i, x, y).wait_send()
 
     @pl.loop(0, STRATA - 1)
     def _(s):
@@ -279,15 +328,6 @@
         (ret_copy_down(p) if p in DOWN else ret_copy(p)).wait_send()
     for p in DOWN:
         relay_copy(p).wait_send()
-
-    @pl.when(z < 3)
-    def _():
-        for p in order:
-            turn_copy(p).wait_send()
-
-    store_u.wait()
-    for store in stores:
-        store.wait()
 
 
 def body(observed, block_mask, plan, cell_factors, region_factors):
@@ -297,7 +337,7 @@
     dma = pltpu.SemaphoreType.DMA
     f32, bf16 = jnp.float32, jnp.bfloat16
     anywhere = pl.BlockSpec(memory_space=pl.ANY)
-    out = jax.ShapeDtypeStruct((ROWS, RANK), f32)
+    out = pltpu.VMEM((ROWS, RANK), f32)
     return pl.pallas_call(
         functools.partial(kernel, scale, rate),
         name="epoch",
@@ -309,10 +349,10 @@
             anywhere,
             anywhere,
         ],
-        out_specs=(anywhere, anywhere),
+        out_specs=(pl.BlockSpec(memory_space=pltpu.VMEM),) * 2,
         scratch_shapes=[
             pltpu.VMEM((STRATA, ROWS, ROWS), bf16),
-            pltpu.VMEM((10, ROWS, RANK), f32),
+            pltpu.VMEM((9, ROWS, RANK), f32),
             pltpu.VMEM((STRATA + 1, ROWS, RANK), f32),
             pltpu.VMEM((STRATA, ROWS, RANK), f32),
             pltpu.VMEM((STRATA, HALF, RANK), f32),
@@ -335,17 +375,14 @@
             dma((STRATA, 8)),
             dma((STRATA, 8)),
             dma((RETS,)),
-            dma((2, RETS)),
             dma((RETS,)),
             dma((RETS,)),
             dma((RETS,)),
-            dma((RETS,)),
-            dma((RETS + 1,)),
         ],
         compiler_params=pltpu.CompilerParams(
             collective_id=0, has_side_effects=True, vmem_limit_bytes=56 * 2**20
         ),
-    )(plan, block_mask, observed, cell_factors, region_factors)
+    )(plan, block_mask.T, observed, cell_factors, region_factors)
 
 
 def solution(mesh):

time: 164 us -> 143 us (0.87)
  Pallas kernels: 156 us -> 139 us
  local copies, waits for them, and re-layouts: 5.97 us -> 1.94 us
    pallas_call x1, Pallas kernels: 156 us -> 139 us  [body(): pl.pallas_call(functools.partial(kernel, scale, rate), name='epoch', out_...]
    unnamed x3 -> x2, local copies, waits for them, and re-layouts: 5.97 us -> 1.94 us
where the time goes in v2:
time: 143 us; the launch traced here: 142 us
  Pallas kernels  139 us (97%)
  local copies, waits for them, and re-layouts  1.94 us (1%)
    pallas_call x1, Pallas kernels, body(): pl.pallas_call(functools.partial(kernel, scale, rate), name='epoch', out_...  139 us

profile of v2, /device:TPU:73, one launch (start us, length us, event | category | flops | bytes accessed | tf_op | source)
XLA Modules:
  0.0 142.1 jit_solution(9025708549896561893)
XLA Ops:
  0.6 139.5 %epoch.1 = (f32[1024,256]{1,0:T(8,128)S(1)}, f32[1024,256]{1,0:T(8,128)S(1)}) custom-call(s32[4]{0:T(128)} %plan.1, s32[32,128]{1,0:T(8,128)} %bitcast.1, bf16[1024,4096]{1,0:T(8,128)(2,1)} %y_hbm.1, f32[1024,256]{1,0:T(8,128)} %u_hbm.1, f32[1024,256]{1,0:T(8,128)} %v_hbm.1), custom_call_target="tpu_custom_call" | custom-call | tf_op jit(solution)/shard_map/epoch/pallas_call | solution.py:341
  140.1 1.0 copy.9
  141.1 1.0 copy.10

commit v3 on v2

--- a/solution.py
+++ b/solution.py
@@ -18,8 +18,10 @@
 PIECE = 64
 RET = 128
 RETS = ROWS // RET
+ROUTES = "PDPD"
 DOWN = (0, 2, 4)
-RAW, FINAL, RELAY = 4, 7, 8
+TURNS = (5, 7)
+RAW, FINAL, RELAY, TURN = 4, 7, 8, 9
 NT = (((1,), (1,)), ((), ()))
 TN = (((0,), (0,)), ((), ()))
 
@@ -40,7 +42,7 @@
     ybuf, vbuf, ubuf, gbuf, core_buf, sum_buf, expanded, resid, u_bf, u_scaled, moment,
     load_sem, shift_send, shift_recv, pass_send,
     core_send, core_recv, rs_send, rs_recv, ag_send, ag_recv, agc_send, agc_recv,
-    ret_send, ret_recv, relay_send, relay_recv,
+    ret_send, ret_recv, relay_send, relay_recv, turn_send,
 ):
     cell, region = lax.axis_index("cell"), lax.axis_index("region")
     z, core, chip = cell % 8, region % 2, region // 2
@@ -78,6 +80,7 @@
     last = (cell + 13) % 16
     sender = last - last % 8 + (last % 8 + 5) % 8
     greeted += [((cell + 3) % 16, region), ((along(3) + 3) % 16, region)]
+    greeted += [((cell + 15) % 16, region), ((cell + 1) % 16, region)]
     greeted += [(last, region), (sender, region)]
     for c, r in greeted:
         pl.semaphore_signal(
@@ -98,9 +101,10 @@
     mine = core * HALF + chip * PIECE
 
     def shift_copy(s, k):
-        slot = s + 1 + is0 * (RAW - 1)
-        first = along(-1)
-        to = first if k < 2 else first + is0 * (across - first)
+        near = along(-1)
+        next_cell = (cell + 15) % 16
+        slot = s + 1 if ROUTES[k] == "D" else s + 1 + is0 * (RAW - 1)
+        to = {"D": next_cell, "Q": near, "P": near + is0 * (across - near)}[ROUTES[k]]
         return remote(v_rows(s, k), v_rows(slot, k), shift_send.at[s, k], shift_recv.at[slot, k], to, region)
 
     def shift_copy_in(s, k):
@@ -114,18 +118,28 @@
         remote(v_rows(RAW + s, k), v_rows(s + 1, k), pass_send.at[s, k], shift_recv.at[s + 1, k], to, region).wait_send()
 
     def ret_copy(p):
-        return remote(ret_rows(3, p), ret_rows(FINAL, p), ret_send.at[p], ret_recv.at[p], (cell + 3) % 16, region)
+        home = (cell + 3) % 16
+        turns = (z + 3) // 8 if p in TURNS else 0
+        slot, to = FINAL + turns * (TURN - FINAL), home + turns * (across - home)
+        return remote(ret_rows(3, p), ret_rows(slot, p), ret_send.at[p], ret_recv.at[turns, p], to, region)
+
+    def turn_in(p):
+        rows = ret_rows(TURN, p)
+        return remote(rows, rows, ret_send.at[p], ret_recv.at[1, p], cell, region)
+
+    def turn_copy(p):
+        return remote(ret_rows(TURN, p), ret_rows(FINAL, p), turn_send.at[p], ret_recv.at[0, p], along(3), region)
 
     def ret_copy_down(p):
         return remote(ret_rows(3, p), ret_rows(RELAY, p), ret_send.at[p], relay_recv.at[p], along(-3), region)
 
     def relay_copy(p):
         home = (along(3) + 3) % 16
-        return remote(ret_rows(RELAY, p), ret_rows(FINAL, p), relay_send.at[p], ret_recv.at[p], home, region)
+        return remote(ret_rows(RELAY, p), ret_rows(FINAL, p), relay_send.at[p], ret_recv.at[0, p], home, region)
 
     def ret_in(p):
         rows = ret_rows(FINAL, p)
-        return remote(rows, rows, ret_send.at[p], ret_recv.at[p], cell, region)
+        return remote(rows, rows, ret_send.at[p], ret_recv.at[0, p], cell, region)
 
     def core_copy(s):
         away = pl.ds((1 - core) * HALF, HALF)
@@ -246,25 +260,17 @@
         reduce_core(s)
         reduce_far(s)
 
-        @pl.when(z == 7)
+        @pl.when(z == 0)
         def _():
-            pass_on(s, 0, across)
+            pass_on(s, 0, along(-1))
+
+        reduce_near(s)
+
+        gather_y(s)
 
         @pl.when(z == 0)
         def _():
             pass_on(s, 2, along(-1))
-
-        reduce_near(s)
-
-        @pl.when(z == 7)
-        def _():
-            pass_on(s, 1, across)
-
-        gather_y(s)
-
-        @pl.when(z == 0)
-        def _():
-            pass_on(s, 3, along(-1))
 
         gather(s)
 
@@ -276,6 +282,12 @@
         for p in (2 * k, 2 * k + 1):
             (ret_copy_down(p) if p in DOWN else ret_copy(p)).start()
     reduce_core(s)
+
+    @pl.when(z >= 5)
+    def _():
+        for p in TURNS:
+            turn_in(p).wait_recv()
+            turn_copy(p).start()
 
     def relay(p):
         ret_copy_down(p).wait_recv()
@@ -314,20 +326,20 @@
         for k in range(CHUNKS):
             shift_copy(s, k).wait_send()
 
-        @pl.when(z == 7)
-        def _():
-            pass_wait(s, 0, across)
-            pass_wait(s, 1, across)
-
         @pl.when(z == 0)
         def _():
+            pass_wait(s, 0, along(-1))
             pass_wait(s, 2, along(-1))
-            pass_wait(s, 3, along(-1))
 
     for p in range(RETS):
         (ret_copy_down(p) if p in DOWN else ret_copy(p)).wait_send()
     for p in DOWN:
         relay_copy(p).wait_send()
+
+    @pl.when(z >= 5)
+    def _():
+        for p in TURNS:
+            turn_copy(p).wait_send()
 
 
 def body(observed, block_mask, plan, cell_factors, region_factors):
@@ -352,7 +364,7 @@
         out_specs=(pl.BlockSpec(memory_space=pltpu.VMEM),) * 2,
         scratch_shapes=[
             pltpu.VMEM((STRATA, ROWS, ROWS), bf16),
-            pltpu.VMEM((9, ROWS, RANK), f32),
+            pltpu.VMEM((10, ROWS, RANK), f32),
             pltpu.VMEM((STRATA + 1, ROWS, RANK), f32),
             pltpu.VMEM((STRATA, ROWS, RANK), f32),
             pltpu.VMEM((STRATA, HALF, RANK), f32),
@@ -375,6 +387,7 @@
             dma((STRATA, 8)),
             dma((STRATA, 8)),
             dma((RETS,)),
+            dma((2, RETS)),
             dma((RETS,)),
             dma((RETS,)),
             dma((RETS,)),

time: 143 us -> 135 us (0.944)
  Pallas kernels: 139 us -> 132 us
    pallas_call x1, Pallas kernels: 139 us -> 132 us  [body(): pl.pallas_call(functools.partial(kernel, scale, rate), name='epoch', out_...]
where the time goes in v3:
time: 135 us
  Pallas kernels  132 us (98%)
  local copies, waits for them, and re-layouts  1.94 us (1%)
    pallas_call x1, Pallas kernels, body(): pl.pallas_call(functools.partial(kernel, scale, rate), name='epoch', out_...  132 us

profile of v3, /device:TPU:73, one launch (start us, length us, event | category | flops | bytes accessed | tf_op | source)
XLA Modules:
  0.0 134.9 jit_solution(14703663044943341875)
XLA Ops:
  0.6 132.3 %epoch.1 = (f32[1024,256]{1,0:T(8,128)S(1)}, f32[1024,256]{1,0:T(8,128)S(1)}) custom-call(s32[4]{0:T(128)} %plan.1, s32[32,128]{1,0:T(8,128)} %bitcast.1, bf16[1024,4096]{1,0:T(8,128)(2,1)} %y_hbm.1, f32[1024,256]{1,0:T(8,128)} %u_hbm.1, f32[1024,256]{1,0:T(8,128)} %v_hbm.1), custom_call_target="tpu_custom_call" | custom-call | tf_op jit(solution)/shard_map/epoch/pallas_call | solution.py:353
  133.0 1.0 copy.9
  134.0 1.0 copy.10

commit v4 on v3

--- a/solution.py
+++ b/solution.py
@@ -95,7 +95,6 @@
         expanded[q] = lax.dot_general(mask_bf, chosen, TN, preferred_element_type=jnp.float32)
     for load in loads:
         load.wait()
-    pl.semaphore_wait(barrier, len(greeted))
 
     is0 = 1 - (z + 7) // 8
     mine = core * HALF + chip * PIECE
@@ -256,6 +255,11 @@
             def _():
                 shift_copy_in(s, k)
             chunk(s, k)
+            if k == 0:
+                @pl.when(s == 0)
+                def _():
+                    pl.semaphore_wait(barrier, len(greeted))
+
             shift_copy(s, k).start()
         reduce_core(s)
         reduce_far(s)

time: 135 us -> 134 us (level)
  no operation moved by 1% of the time
where the time goes in v4:
time: 134 us
  Pallas kernels  131 us (98%)
  local copies, waits for them, and re-layouts  1.94 us (1%)
    pallas_call x1, Pallas kernels, body(): pl.pallas_call(functools.partial(kernel, scale, rate), name='epoch', out_...  131 us

profile of v4, /device:TPU:73, one launch (start us, length us, event | category | flops | bytes accessed | tf_op | source)
XLA Modules:
  0.0 134.1 jit_solution(10612004638027322447)
XLA Ops:
  0.6 131.5 %epoch.1 = (f32[1024,256]{1,0:T(8,128)S(1)}, f32[1024,256]{1,0:T(8,128)S(1)}) custom-call(s32[4]{0:T(128)} %plan.1, s32[32,128]{1,0:T(8,128)} %bitcast.1, bf16[1024,4096]{1,0:T(8,128)(2,1)} %y_hbm.1, f32[1024,256]{1,0:T(8,128)} %u_hbm.1, f32[1024,256]{1,0:T(8,128)} %v_hbm.1), custom_call_target="tpu_custom_call" | custom-call | tf_op jit(solution)/shard_map/epoch/pallas_call | solution.py:357
  132.1 1.0 copy.9
  133.1 1.0 copy.10
